TPU v7x, 128 devices: a whole 4x4x4 slice. The times are simulated.
128 devices in a mesh: dp: 32 (over z, y, x_hi), mod: 4 (over x_lo, core).
Axes of the slice: x: 4 (x_hi: 2, x_lo: 2; x = x_hi * 2 + x_lo), y: 4, z: 4, core: 2. Of those that a mesh axis runs over, the one named last changes fastest.
Arguments:
- embeddings: bfloat16 [4, 8192, 512], P('mod', 'dp'), may hold values from -4 to 4
- pairings: int32 [3, 4], replicated, may hold values from 0 to 3, as said below
- logit_scale: float32 [3], replicated, may hold values from 2 to 6
Outputs:
- gradient: float32 [4, 8192, 512], P('mod', 'dp')
- losses: float32 [4, 8192], P('mod', 'dp')
Inputs may be any that keep to these rules, and one draw needn't show every extreme that they name: Row k of pairings maps each modality to its partner in matching k; each row is an involution without fixed points, and the three rows are the three perfect matchings of the four modalities in some order.
All inputs are finite; a program needn't handle non-finite values.
Results may differ from a plain program's by a relative error of at most 0.0013.
Values may be sent and summed in bfloat16 or wider, within the bound.
A program may use at most 192 MiB of HBM per device.

v0:
```python
import jax
import jax.numpy as jnp
from jax import lax
from jax.sharding import PartitionSpec as P


def shards(embeddings, pairings, logit_scale):
    row_count = embeddings.shape[1]
    feat_width = embeddings.shape[2]
    mod_index = lax.axis_index("mod")
    anchor = embeddings[0]
    local_set = lax.all_gather(embeddings, "mod", axis=0, tiled=True)
    gradient = jnp.zeros((row_count, feat_width), jnp.float32)
    losses = jnp.zeros((row_count,), jnp.float32)
    for matching in range(3):
        partner_id = pairings[matching][mod_index]
        factor = logit_scale[matching]
        own_rows = lax.dynamic_index_in_dim(local_set, partner_id, 0, keepdims=False)
        partner = lax.all_gather(own_rows, "dp", axis=0, tiled=True)
        scores = factor * lax.dot_general(
            anchor, partner, (((1,), (1,)), ((), ())), preferred_element_type=jnp.float32
        )
        row_max = jnp.max(scores, 1, keepdims=True)
        row_lse = row_max[:, 0] + jnp.log(jnp.sum(jnp.exp(scores - row_max), 1))
        col_max = lax.pmax(jnp.max(scores, 0).astype(jnp.bfloat16), "dp").astype(jnp.float32)
        col_sum = lax.psum(jnp.sum(jnp.exp(scores - col_max[None, :]), 0), "dp")
        col_lse = col_max + jnp.log(col_sum)
        weights = (jnp.exp(scores - row_lse[:, None]) + jnp.exp(scores - col_lse[None, :])).astype(
            jnp.bfloat16
        )
        product = jnp.dot(weights, partner, preferred_element_type=jnp.float32)
        own_float = own_rows.astype(jnp.float32)
        diagonal = factor * jnp.sum(anchor.astype(jnp.float32) * own_float, -1)
        gradient = gradient + factor * (product - 2.0 * own_float)
        losses = losses + (row_lse - diagonal)
    return (gradient[None], losses[None])


def solution(mesh):
    return jax.shard_map(
        shards,
        mesh=mesh,
        in_specs=(P("mod", "dp", None), P(), P()),
        out_specs=(P("mod", "dp", None), P("mod", "dp")),
        check_vma=False,
    )
```

profile of v0, /device:TPU:0, one launch (start us, length us, event | category | flops | bytes accessed | tf_op | source)
XLA Modules:
  0.0 907.2 jit_solution(15729852674671141056)
XLA Ops:
  7.2 0.7 all-gather.8.cloned.1.call-update
  7.9 0.8 fusion.51
  16.0 16.9 %all-gather.8.cloned.1.call-done = bf16[4,256,512]{2,1,0:T(8,128)(2,1)} async-done(((bf16[1,256,512]{2,1,0:T(8,128)(2,1)}), bf16[4,256,512]{2,1,0:T(8,128)(2,1)}) %all-gather.8.cloned.1.call-update) | async-done | bytes 1048592 | tf_op jit(solution)/shard_map/all_gather | solution.py:12
  32.8 2.1 fusion.42
  35.0 0.7 all-gather.10.cloned.1.call-update
  36.3 1.4 fusion.52
  37.7 103.0 %all-gather.14.cloned.1.call-done = bf16[1,8192,512]{2,1,0:T(8,128)(2,1)} async-done(((bf16[1,256,512]{2,1,0:T(8,128)(2,1)}), bf16[1,8192,512]{2,1,0:T(8,128)(2,1)}) %all-gather.14.cloned.1.call-update) | async-done | bytes 8388624 | tf_op jit(solution)/shard_map/all_gather | solution.py:19
  140.8 9.6 %fusion.50 = (f32[256]{0:T(256)S(1)}, bf16[8192]{0:T(1024)(128)(2,1)S(1)}, f32[8192,256]{1,0:T(8,128)}) fusion(bf16[1,256,512]{2,1,0:T(8,128)(2,1)} %param.3, bf16[1,8192,512]{2,1,0:T(8,128)(2,1)} %all-gather.14.cloned.1.call-done, f32[]{:T(128)} %bitcast.9), kind=kOutput, calls=%fused_computation.63 | convolution fusion | flops 2153766656 | bytes 17056772 | tf_op jit(solution)/shard_map/dot_general | solution.py:20
  150.4 95.9 %all-gather.10.cloned.1.call-done = bf16[1,8192,512]{2,1,0:T(8,128)(2,1)} async-done(((bf16[1,256,512]{2,1,0:T(8,128)(2,1)}), bf16[1,8192,512]{2,1,0:T(8,128)(2,1)}) %all-gather.10.cloned.1.call-update) | async-done | bytes 8388624 | tf_op jit(solution)/shard_map/all_gather | solution.py:19
  246.2 9.6 %fusion.48 = (f32[256]{0:T(256)S(1)}, bf16[8192]{0:T(1024)(128)(2,1)S(1)}, f32[8192,256]{1,0:T(8,128)}) fusion(bf16[1,256,512]{2,1,0:T(8,128)(2,1)S(1)} %copy-done.1, bf16[1,8192,512]{2,1,0:T(8,128)(2,1)} %all-gather.10.cloned.1.call-done, f32[]{:T(128)} %bitcast), kind=kOutput, calls=%fused_computation.61 | convolution fusion | flops 2153766656 | bytes 17056772 | tf_op jit(solution)/shard_map/dot_general | solution.py:20
  255.9 95.1 %all-gather.12.cloned.1.call-done = bf16[1,8192,512]{2,1,0:T(8,128)(2,1)} async-done(((bf16[1,256,512]{2,1,0:T(8,128)(2,1)}), bf16[1,8192,512]{2,1,0:T(8,128)(2,1)}) %all-gather.12.cloned.1.call-update) | async-done | bytes 8388624 | tf_op jit(solution)/shard_map/all_gather | solution.py:19
  351.0 9.6 %fusion.49 = (f32[256]{0:T(256)S(1)}, bf16[8192]{0:T(1024)(128)(2,1)S(1)}, f32[8192,256]{1,0:T(8,128)}) fusion(bf16[1,256,512]{2,1,0:T(8,128)(2,1)S(1)} %copy-done.1, bf16[1,8192,512]{2,1,0:T(8,128)(2,1)} %all-gather.12.cloned.1.call-done, f32[]{:T(128)} %bitcast.5), kind=kOutput, calls=%fused_computation.62 | convolution fusion | flops 2153766656 | bytes 17056772 | tf_op jit(solution)/shard_map/dot_general | solution.py:20
  360.6 180.2 %all-reduce.1 = (bf16[8192]{0:T(1024)(128)(2,1)S(1)}, bf16[8192]{0:T(1024)(128)(2,1)S(1)}, bf16[8192]{0:T(1024)(128)(2,1)S(1)}) all-reduce(bf16[8192]{0:T(1024)(128)(2,1)S(1)} %get-tuple-element.13, bf16[8192]{0:T(1024)(128)(2,1)S(1)} %get-tuple-element.9, ...), channel_id=1, replica_groups=mesh['dp'=32,'mod'=4] {'dp'}, use_global_device_ids=true, to_apply=%region_15.16 | all-reduce | flops 24576 | bytes 98304 | tf_op jit(solution)/shard_map/pmax | solution.py:25
  540.9 7.0 exponential_reduce_fusion.5
  547.8 4.2 exponential_reduce_fusion.3
  552.0 4.2 exponential_reduce_fusion.1
  556.2 2.4 subtract_add_fusion
  558.6 312.2 %all-reduce.4.cloned.1.call-done = (f32[8192]{0:T(1024)}, f32[8192]{0:T(1024)}, f32[8192]{0:T(1024)}) async-done(((f32[8192]{0:T(1024)}, f32[8192]{0:T(1024)}, f32[8192]{0:T(1024)}), (f32[8192]{0:T(1024)}, f32[8192]{0:T(1024)}, f32[8192]{0:T(1024)})) %all-reduce.4.cloned.1.call-update) | async-done | bytes 98320 | tf_op jit(solution)/shard_map/psum | solution.py:26
  870.8 0.8 log_add_fusion.2
  871.6 0.8 log_add_fusion.1
  872.4 0.8 log_add_fusion
  873.2 10.3 %fusion.33 = f32[256,512]{1,0:T(8,128)S(1)} fusion(bf16[1,8192,512]{2,1,0:T(8,128)(2,1)} %all-gather.12.cloned.1.call-done, f32[8192,256]{1,0:T(8,128)} %get-tuple-element.37, f32[8192]{0:T(1024)S(1)} %log_add_fusion.1, f32[256]{0:T(256)S(1)} %get-tuple-element.25, bf16[1,256,512]{2,1,0:T(8,128)(2,1)S(1)} %copy-done.4, f32[]{:T(128)} %bitcast.5), kind=kOutput, calls=%fused_computation.33 | convolution fusion | flops 2156396544 | bytes 17597444 | tf_op jit(solution)/shard_map/dot_general | solution.py:31
  883.5 10.4 %fusion.39 = f32[256,512]{1,0:T(8,128)S(1)} fusion(bf16[1,8192,512]{2,1,0:T(8,128)(2,1)} %all-gather.14.cloned.1.call-done, f32[8192,256]{1,0:T(8,128)} %get-tuple-element.36, f32[8192]{0:T(1024)S(1)} %log_add_fusion, f32[256]{0:T(256)S(1)} %get-tuple-element.26, bf16[1,256,512]{2,1,0:T(8,128)(2,1)S(1)} %copy-done.3, f32[]{:T(128)} %bitcast.9), kind=kOutput, calls=%fused_computation.35 | convolution fusion | flops 2156396544 | bytes 17597444 | tf_op jit(solution)/shard_map/dot_general | solution.py:31
  894.0 6.7 fusion.27
  (38 shorter events, 2.1 us)
Async XLA Ops:
  7.2 25.7 %all-gather.8.cloned.1.call-start = ((), (), s32[]{:S(2)}) async-start(), calls=%async_computation | async-start | bytes 1310720 | tf_op jit(solution)/shard_map/all_gather | solution.py:12
  7.9 132.9 %all-gather.14.cloned.1.call-start = ((), (), s32[]{:S(2)}) async-start(), calls=%async_computation.3 | async-start | bytes 8650752 | tf_op jit(solution)/shard_map/all_gather | solution.py:19
  35.0 211.3 %all-gather.10.cloned.1.call-start = ((), (), s32[]{:S(2)}) async-start(), calls=%async_computation.1 | async-start | bytes 8650752 | tf_op jit(solution)/shard_map/all_gather | solution.py:19
  35.7 315.3 %all-gather.12.cloned.1.call-start = ((), (), s32[]{:S(2)}) async-start(), calls=%async_computation.2 | async-start | bytes 8650752 | tf_op jit(solution)/shard_map/all_gather | solution.py:19
  36.3 834.6 %all-reduce.4.cloned.1.call-start = ((), (), s32[]{:S(2)}) async-start(), calls=%async_computation.4 | async-start | bytes 196608 | tf_op jit(solution)/shard_map/psum | solution.py:26
  140.7 105.5 %copy-start.1 = (bf16[1,256,512]{2,1,0:T(8,128)(2,1)S(1)}, bf16[1,256,512]{2,1,0:T(8,128)(2,1)}, u32[]{:S(2)}) copy-start(bf16[1,256,512]{2,1,0:T(8,128)(2,1)} %param.3) | copy-start | bytes 786436
  540.8 7.0 copy-start
  540.9 11.2 %slice-start = ((s8[8388608]{0:T(1024)(128)(4,1)}), s8[4194304]{0:T(1024)(128)(4,1)S(1)}, s32[]{:S(2)}) async-start(s8[8388608]{0:T(1024)(128)(4,1)} %bitcast.76), calls=%async_computation.5 | async-start | bytes 8388608
  547.8 4.2 slice-start.1
  547.8 325.3 %copy-start.4 = (bf16[1,256,512]{2,1,0:T(8,128)(2,1)S(1)}, bf16[1,256,512]{2,1,0:T(8,128)(2,1)}, u32[]{:S(2)}) copy-start(bf16[1,256,512]{2,1,0:T(8,128)(2,1)} %get-tuple-element.28) | copy-start | bytes 786436
  873.2 10.3 %copy-start.3 = (bf16[1,256,512]{2,1,0:T(8,128)(2,1)S(1)}, bf16[1,256,512]{2,1,0:T(8,128)(2,1)}, u32[]{:S(2)}) copy-start(bf16[1,256,512]{2,1,0:T(8,128)(2,1)} %get-tuple-element.29) | copy-start | bytes 786436
  873.2 20.7 %slice-start.2 = ((s8[8388608]{0:T(1024)(128)(4,1)}), s8[4194304]{0:T(1024)(128)(4,1)S(1)}, s32[]{:S(2)}) async-start(s8[8388608]{0:T(1024)(128)(4,1)} %bitcast.78), calls=%async_computation.7 | async-start | bytes 8388608
  873.2 20.7 %slice-start.4 = ((s8[8388608]{0:T(1024)(128)(4,1)}), s8[4194304]{0:T(1024)(128)(4,1)S(1)}, s32[]{:S(2)}) async-start(s8[8388608]{0:T(1024)(128)(4,1)} %bitcast.81), calls=%async_computation.9 | async-start | bytes 8388608
  883.5 10.5 %slice-start.3 = ((s8[8388608]{0:T(1024)(128)(4,1)}), s8[4194304]{0:T(1024)(128)(4,1)S(1)}, s32[]{:S(2)}) async-start(s8[8388608]{0:T(1024)(128)(4,1)} %bitcast.78), calls=%async_computation.8 | async-start | bytes 8388608
  883.5 10.5 %slice-start.5 = ((s8[8388608]{0:T(1024)(128)(4,1)}), s8[4194304]{0:T(1024)(128)(4,1)S(1)}, s32[]{:S(2)}) async-start(s8[8388608]{0:T(1024)(128)(4,1)} %bitcast.81), calls=%async_computation.10 | async-start | bytes 8388608
  883.5 10.4 %copy-start.2 = (bf16[1,256,512]{2,1,0:T(8,128)(2,1)S(1)}, bf16[1,256,512]{2,1,0:T(8,128)(2,1)}, u32[]{:S(2)}) copy-start(bf16[1,256,512]{2,1,0:T(8,128)(2,1)} %get-tuple-element.27) | copy-start | bytes 786436
Sparse Core Ops, SparseCore 0:
  9.7 23.1 all-gather.7
  35.9 104.8 all-gather.13
  144.4 101.7 all-gather.9
  249.2 101.7 all-gather.11
  556.3 314.4 all-reduce.3
where the time goes:
time: 908 us; the launch traced here: 907 us
  waiting for transfers between devices  625 us (69%)
  blocking collectives  180 us (20%)
  matrix products  56.1 us (6%)
  other arithmetic  22.1 us (2%)
  between operations  19.9 us (2%)
    psum x1, waiting for transfers between devices, shards(): col_sum = lax.psum(jnp.sum(jnp.exp(scores - col_max[None, :]), 0), 'dp')  312 us
    all_gather x3, waiting for transfers between devices, shards(): partner = lax.all_gather(own_rows, 'dp', axis=0, tiled=True)  294 us
    pmax x1, blocking collectives, shards(): lax.pmax(jnp.max(scores, 0).astype(jnp.bfloat16), 'dp').astype(jnp.float32)  180 us
    dot_general x3, matrix products, shards(): lax.dot_general(anchor, partner, (((1,), (1,)), ((), ())), preferred_elem...  28.8 us
    dot_general x3, matrix products, shards(): product = jnp.dot(weights, partner, preferred_element_type=jnp.float32)  27.3 us
  transfers between devices with their start and end apart: 5, of which 5 were waited for; matrix products, arithmetic and copies ran while one was open for 3% of the time, Pallas kernels for 0%

commit v1 on v0

--- a/solution.py
+++ b/solution.py
@@ -23,7 +23,9 @@
         row_max = jnp.max(scores, 1, keepdims=True)
         row_lse = row_max[:, 0] + jnp.log(jnp.sum(jnp.exp(scores - row_max), 1))
         col_max = lax.pmax(jnp.max(scores, 0).astype(jnp.bfloat16), "dp").astype(jnp.float32)
-        col_sum = lax.psum(jnp.sum(jnp.exp(scores - col_max[None, :]), 0), "dp")
+        col_sum = jnp.sum(
+            lax.all_gather(jnp.sum(jnp.exp(scores - col_max[None, :]), 0), "dp"), axis=0
+        )
         col_lse = col_max + jnp.log(col_sum)
         weights = (jnp.exp(scores - row_lse[:, None]) + jnp.exp(scores - col_lse[None, :])).astype(
             jnp.bfloat16

time: 908 us -> 780 us (0.86)
  waiting for transfers between devices: 625 us -> 490 us
    psum x1 -> x0, waiting for transfers between devices: 312 us -> none  [shards(): col_sum = lax.psum(jnp.sum(jnp.exp(scores - col_max[None, :]), 0), 'dp')]
    all_gather x0 -> x3, waiting for transfers between devices: none -> 177 us  [shards(): lax.all_gather(jnp.sum(jnp.exp(scores - col_max[None, :]), 0), 'dp')]
  transfers between devices with their start and end apart: 5 -> 7, of which waited for: 5 -> 7; matrix products, arithmetic and copies ran while one was open for 3% -> 5% of each run, Pallas kernels for 0% -> 0%
where the time goes in v1:
time: 780 us
  waiting for transfers between devices  490 us (63%)
  blocking collectives  180 us (23%)
  matrix products  56.1 us (7%)
  other arithmetic  25.5 us (3%)
  between operations  20.3 us (3%)
    all_gather x3, waiting for transfers between devices, shards(): partner = lax.all_gather(own_rows, 'dp', axis=0, tiled=True)  294 us
    pmax x1, blocking collectives, shards(): lax.pmax(jnp.max(scores, 0).astype(jnp.bfloat16), 'dp').astype(jnp.float32)  180 us
    all_gather x3, waiting for transfers between devices, shards(): lax.all_gather(jnp.sum(jnp.exp(scores - col_max[None, :]), 0), 'dp')  177 us
    dot_general x3, matrix products, shards(): lax.dot_general(anchor, partner, (((1,), (1,)), ((), ())), preferred_elem...  28.9 us
    dot_general x3, matrix products, shards(): product = jnp.dot(weights, partner, preferred_element_type=jnp.float32)  27.3 us
    reduce_sum x3, other arithmetic, shards(): row_lse = row_max[:, 0] + jnp.log(jnp.sum(jnp.exp(scores - row_max), 1))  20.5 us
    all_gather x1, waiting for transfers between devices, shards(): local_set = lax.all_gather(embeddings, 'mod', axis=0, tiled=True)  16.9 us
  transfers between devices with their start and end apart: 7, of which 7 were waited for; matrix products, arithmetic and copies ran while one was open for 5% of the time, Pallas kernels for 0%

profile of v1, /device:TPU:0, one launch (start us, length us, event | category | flops | bytes accessed | tf_op | source)
XLA Modules:
  0.0 779.9 jit_solution(16044548772414712375)
XLA Ops:
  7.9 0.8 fusion.51
  16.0 16.9 %all-gather.14.cloned.1.call-done = bf16[4,256,512]{2,1,0:T(8,128)(2,1)} async-done(((bf16[1,256,512]{2,1,0:T(8,128)(2,1)}), bf16[4,256,512]{2,1,0:T(8,128)(2,1)}) %all-gather.14.cloned.1.call-update) | async-done | bytes 1048592 | tf_op jit(solution)/shard_map/all_gather | solution.py:12
  32.8 2.1 fusion.42
  36.3 1.4 fusion.52
  37.7 103.0 %all-gather.24.cloned.1.call-done = bf16[1,8192,512]{2,1,0:T(8,128)(2,1)} async-done(((bf16[1,256,512]{2,1,0:T(8,128)(2,1)}), bf16[1,8192,512]{2,1,0:T(8,128)(2,1)}) %all-gather.24.cloned.1.call-update) | async-done | bytes 8388624 | tf_op jit(solution)/shard_map/all_gather | solution.py:19
  140.8 9.7 %fusion.50 = (f32[256]{0:T(256)S(1)}, bf16[8192]{0:T(1024)(128)(2,1)S(1)}, f32[8192,256]{1,0:T(8,128)}) fusion(bf16[1,256,512]{2,1,0:T(8,128)(2,1)} %param.3, bf16[1,8192,512]{2,1,0:T(8,128)(2,1)} %all-gather.24.cloned.1.call-done, f32[]{:T(128)} %bitcast.9), kind=kOutput, calls=%fused_computation.63 | convolution fusion | flops 2153766656 | bytes 17056772 | tf_op jit(solution)/shard_map/dot_general | solution.py:20
  150.4 95.2 %all-gather.20.cloned.1.call-done = bf16[1,8192,512]{2,1,0:T(8,128)(2,1)} async-done(((bf16[1,256,512]{2,1,0:T(8,128)(2,1)}), bf16[1,8192,512]{2,1,0:T(8,128)(2,1)}) %all-gather.20.cloned.1.call-update) | async-done | bytes 8388624 | tf_op jit(solution)/shard_map/all_gather | solution.py:19
  245.7 9.6 %fusion.49 = (f32[256]{0:T(256)S(1)}, bf16[8192]{0:T(1024)(128)(2,1)S(1)}, f32[8192,256]{1,0:T(8,128)}) fusion(bf16[1,256,512]{2,1,0:T(8,128)(2,1)S(1)} %copy-done, bf16[1,8192,512]{2,1,0:T(8,128)(2,1)} %all-gather.20.cloned.1.call-done, f32[]{:T(128)} %bitcast.5), kind=kOutput, calls=%fused_computation.62 | convolution fusion | flops 2153766656 | bytes 17056772 | tf_op jit(solution)/shard_map/dot_general | solution.py:20
  255.3 95.7 %all-gather.16.cloned.1.call-done = bf16[1,8192,512]{2,1,0:T(8,128)(2,1)} async-done(((bf16[1,256,512]{2,1,0:T(8,128)(2,1)}), bf16[1,8192,512]{2,1,0:T(8,128)(2,1)}) %all-gather.16.cloned.1.call-update) | async-done | bytes 8388624 | tf_op jit(solution)/shard_map/all_gather | solution.py:19
  351.0 9.6 %fusion.48 = (f32[256]{0:T(256)S(1)}, bf16[8192]{0:T(1024)(128)(2,1)S(1)}, f32[8192,256]{1,0:T(8,128)}) fusion(bf16[1,256,512]{2,1,0:T(8,128)(2,1)S(1)} %copy-done, bf16[1,8192,512]{2,1,0:T(8,128)(2,1)} %all-gather.16.cloned.1.call-done, f32[]{:T(128)} %bitcast), kind=kOutput, calls=%fused_computation.61 | convolution fusion | flops 2153766656 | bytes 17056772 | tf_op jit(solution)/shard_map/dot_general | solution.py:20
  360.6 180.1 %all-reduce = (bf16[8192]{0:T(1024)(128)(2,1)S(1)}, bf16[8192]{0:T(1024)(128)(2,1)S(1)}, bf16[8192]{0:T(1024)(128)(2,1)S(1)}) all-reduce(bf16[8192]{0:T(1024)(128)(2,1)S(1)} %get-tuple-element.13, bf16[8192]{0:T(1024)(128)(2,1)S(1)} %get-tuple-element.9, ...), channel_id=1, replica_groups=mesh['dp'=32,'mod'=4] {'dp'}, use_global_device_ids=true, to_apply=%region_15.16 | all-reduce | flops 24576 | bytes 98304 | tf_op jit(solution)/shard_map/pmax | solution.py:25
  540.7 6.8 exponential_reduce_fusion.1
  547.6 6.8 exponential_reduce_fusion.3
  554.6 6.9 exponential_reduce_fusion.5
  561.5 2.5 subtract_add_fusion
  564.0 45.5 %all-gather.26.cloned.1.call-done = f32[262144]{0:T(1024)} async-done(((f32[8192]{0:T(1024)}), f32[262144]{0:T(1024)}) %all-gather.26.cloned.1.call-update) | async-done | bytes 1048592 | tf_op jit(solution)/shard_map/all_gather | solution.py:27
  609.5 1.4 reshape.137
  611.0 65.7 %all-gather.22.cloned.1.call-done = f32[262144]{0:T(1024)} async-done(((f32[8192]{0:T(1024)}), f32[262144]{0:T(1024)}) %all-gather.22.cloned.1.call-update) | async-done | bytes 1048592 | tf_op jit(solution)/shard_map/all_gather | solution.py:27
  676.7 1.4 reshape.135
  678.3 65.8 %all-gather.18.cloned.1.call-done = f32[262144]{0:T(1024)} async-done(((f32[8192]{0:T(1024)}), f32[262144]{0:T(1024)}) %all-gather.18.cloned.1.call-update) | async-done | bytes 1048592 | tf_op jit(solution)/shard_map/all_gather | solution.py:27
  744.0 1.4 reshape.133
  745.6 10.3 %fusion.39 = f32[256,512]{1,0:T(8,128)S(1)} fusion(bf16[1,8192,512]{2,1,0:T(8,128)(2,1)} %all-gather.24.cloned.1.call-done, f32[8192,256]{1,0:T(8,128)} %get-tuple-element.33, f32[8192]{0:T(1024)S(1)} %log_add_fusion, f32[256]{0:T(256)S(1)} %get-tuple-element.23, bf16[1,256,512]{2,1,0:T(8,128)(2,1)S(1)} %copy-done.3, f32[]{:T(128)} %bitcast.9), kind=kOutput, calls=%fused_computation.35 | convolution fusion | flops 2156396544 | bytes 17597444 | tf_op jit(solution)/shard_map/dot_general | solution.py:33
  756.0 10.3 %fusion.33 = f32[256,512]{1,0:T(8,128)S(1)} fusion(bf16[1,8192,512]{2,1,0:T(8,128)(2,1)} %all-gather.20.cloned.1.call-done, f32[8192,256]{1,0:T(8,128)} %get-tuple-element.34, f32[8192]{0:T(1024)S(1)} %log_add_fusion.1, f32[256]{0:T(256)S(1)} %get-tuple-element.22, bf16[1,256,512]{2,1,0:T(8,128)(2,1)S(1)} %copy-done.2, f32[]{:T(128)} %bitcast.5), kind=kOutput, calls=%fused_computation.33 | convolution fusion | flops 2156396544 | bytes 17597444 | tf_op jit(solution)/shard_map/dot_general | solution.py:33
  766.4 6.7 fusion.27
  (43 shorter events, 4.0 us)
Async XLA Ops:
  7.2 25.7 %all-gather.14.cloned.1.call-start = ((), (), s32[]{:S(2)}) async-start(), calls=%async_computation | async-start | bytes 1310720 | tf_op jit(solution)/shard_map/all_gather | solution.py:12
  7.9 132.9 %all-gather.24.cloned.1.call-start = ((), (), s32[]{:S(2)}) async-start(), calls=%async_computation.5 | async-start | bytes 8650752 | tf_op jit(solution)/shard_map/all_gather | solution.py:19
  35.0 210.7 %all-gather.20.cloned.1.call-start = ((), (), s32[]{:S(2)}) async-start(), calls=%async_computation.3 | async-start | bytes 8650752 | tf_op jit(solution)/shard_map/all_gather | solution.py:19
  35.7 315.3 %all-gather.16.cloned.1.call-start = ((), (), s32[]{:S(2)}) async-start(), calls=%async_computation.1 | async-start | bytes 8650752 | tf_op jit(solution)/shard_map/all_gather | solution.py:19
  36.3 573.2 %all-gather.26.cloned.1.call-start = ((), (), s32[]{:S(2)}) async-start(), calls=%async_computation.6 | async-start | bytes 1081344 | tf_op jit(solution)/shard_map/all_gather | solution.py:27
  140.7 104.9 %copy-start = (bf16[1,256,512]{2,1,0:T(8,128)(2,1)S(1)}, bf16[1,256,512]{2,1,0:T(8,128)(2,1)}, u32[]{:S(2)}) copy-start(bf16[1,256,512]{2,1,0:T(8,128)(2,1)} %param.3) | copy-start | bytes 786436
  547.5 129.2 %all-gather.22.cloned.1.call-start = ((), (), s32[]{:S(2)}) async-start(), calls=%async_computation.4 | async-start | bytes 1081344 | tf_op jit(solution)/shard_map/all_gather | solution.py:27
  554.4 189.6 %all-gather.18.cloned.1.call-start = ((), (), s32[]{:S(2)}) async-start(), calls=%async_computation.2 | async-start | bytes 1081344 | tf_op jit(solution)/shard_map/all_gather | solution.py:27
  554.6 191.0 %copy-start.3 = (bf16[1,256,512]{2,1,0:T(8,128)(2,1)S(1)}, bf16[1,256,512]{2,1,0:T(8,128)(2,1)}, u32[]{:S(2)}) copy-start(bf16[1,256,512]{2,1,0:T(8,128)(2,1)} %get-tuple-element.26) | copy-start | bytes 786436
  745.6 10.4 %copy-start.2 = (bf16[1,256,512]{2,1,0:T(8,128)(2,1)S(1)}, bf16[1,256,512]{2,1,0:T(8,128)(2,1)}, u32[]{:S(2)}) copy-start(bf16[1,256,512]{2,1,0:T(8,128)(2,1)} %get-tuple-element.25) | copy-start | bytes 786436
  745.6 20.7 %slice-start = ((s8[8388608]{0:T(1024)(128)(4,1)}), s8[4194304]{0:T(1024)(128)(4,1)S(1)}, s32[]{:S(2)}) async-start(s8[8388608]{0:T(1024)(128)(4,1)} %bitcast.76), calls=%async_computation.7 | async-start | bytes 8388608
  745.6 20.7 %slice-start.2 = ((s8[8388608]{0:T(1024)(128)(4,1)}), s8[4194304]{0:T(1024)(128)(4,1)S(1)}, s32[]{:S(2)}) async-start(s8[8388608]{0:T(1024)(128)(4,1)} %bitcast.79), calls=%async_computation.9 | async-start | bytes 8388608
  756.0 10.3 %slice-start.1 = ((s8[8388608]{0:T(1024)(128)(4,1)}), s8[4194304]{0:T(1024)(128)(4,1)S(1)}, s32[]{:S(2)}) async-start(s8[8388608]{0:T(1024)(128)(4,1)} %bitcast.76), calls=%async_computation.8 | async-start | bytes 8388608
  756.0 10.3 %copy-start.1 = (bf16[1,256,512]{2,1,0:T(8,128)(2,1)S(1)}, bf16[1,256,512]{2,1,0:T(8,128)(2,1)}, u32[]{:S(2)}) copy-start(bf16[1,256,512]{2,1,0:T(8,128)(2,1)} %get-tuple-element.24) | copy-start | bytes 786436
  756.0 10.3 %slice-start.3 = ((s8[8388608]{0:T(1024)(128)(4,1)}), s8[4194304]{0:T(1024)(128)(4,1)S(1)}, s32[]{:S(2)}) async-start(s8[8388608]{0:T(1024)(128)(4,1)} %bitcast.79), calls=%async_computation.10 | async-start | bytes 8388608
Sparse Core Ops, SparseCore 0:
  9.7 23.1 all-gather.13
  35.9 104.8 all-gather.23
  143.8 101.7 all-gather.19
  249.2 101.7 all-gather.15
  547.6 61.8 all-gather.25
  612.5 64.1 all-gather.21
  679.8 64.1 all-gather.17
